TPU v7x, 32 devices: a whole 2x2x4 slice. The times are simulated.
32 devices in a mesh: groups: 2 (over y), chol: 4 (over z), walk: 4 (over x, core).
Axes of the slice: x: 2, y: 2, z: 4, core: 2. Of those that a mesh axis runs over, the one named last changes fastest.
Arguments:
- green: bfloat16 [8, 200, 1600], P(('groups', 'walk')), parts along dimension 0, may hold values from -2 to 2
- chol: bfloat16 [16, 200, 1600], P(('groups', 'chol')), parts along dimension 0, may hold values from -0.19921875 to 0.19921875
- trial: bfloat16 [3200, 200], P(('groups', 'chol')), parts along dimension 0, may hold values from -1.1953125 to 1.1953125
- hamil: bfloat16 [1600, 1600], P('chol'), may hold values from -0.21875 to 0.21875
- energy_cot: float32 [8], P('groups'), parts along dimension 0, may hold values from -4 to 4
Outputs:
- d_green: float32 [8, 200, 1600], P(('groups', 'walk'), None, 'chol'), parts along dimension 0
- d_chol: float32 [16, 200, 1600], P(('groups', 'chol'), None, 'walk'), parts along dimension 0
- d_trial: float32 [3200, 200], P(('groups', 'chol')), parts along dimension 0
There are 2 independent parts, one for each index of `groups`. A program takes and returns all parts, laid end to end along the dimension named above; an argument that names none is the same for every part. Nothing has to cross between parts.
All inputs are finite; a program needn't handle non-finite values.
Results may differ from a plain program's by a relative error of at most 0.0029.
Values may be sent and summed in bfloat16 or wider, within the bound.
A program may use at most 64 MiB of HBM per device.

v0:
```python
import jax
import jax.numpy as jnp
from jax import lax
from jax.sharding import PartitionSpec as P


def shards(green, chol, trial, hamil, energy_cot):
    walk_rank = lax.axis_index("walk")
    walk_rows = green.shape[0]
    cot_own = lax.dynamic_slice_in_dim(energy_cot, walk_rank * walk_rows, walk_rows, 0)
    hrot_part = lax.dot_general(
        trial, hamil, (((0,), (0,)), ((), ())), preferred_element_type=jnp.float32
    )
    identity = jnp.eye(trial.shape[1], dtype=jnp.float32)
    quarter = green.shape[2] // lax.axis_size("walk")
    greens = lax.all_gather(green, "walk", axis=0, tiled=True)
    coulomb = jnp.einsum("cip,wip->cw", chol, greens, preferred_element_type=jnp.float32)
    exchange_mat = jnp.einsum("cip,wjp->cwij", chol, greens, preferred_element_type=jnp.float32)
    kernel_mat = (
        energy_cot[None, :, None, None] * (coulomb[:, :, None, None] * identity - exchange_mat)
    ).astype(jnp.bfloat16)
    kernel_own = lax.dynamic_slice_in_dim(kernel_mat, walk_rank * walk_rows, walk_rows, 1)
    green_part = jnp.einsum("cwij,cjp->wip", kernel_own, chol, preferred_element_type=jnp.float32)
    green_part = green_part + cot_own[:, None, None] * hrot_part[None]
    d_green = lax.psum_scatter(green_part, "chol", scatter_dimension=2, tiled=True)
    green_share = lax.dynamic_slice_in_dim(greens, walk_rank * quarter, quarter, 2)
    d_chol = jnp.einsum(
        "cwji,wjp->cip", kernel_mat, green_share, preferred_element_type=jnp.float32
    )
    gbar = jnp.einsum(
        "w,wip->ip",
        energy_cot,
        greens,
        precision=lax.Precision.HIGHEST,
        preferred_element_type=jnp.float32,
    ).astype(jnp.bfloat16)
    d_trial = lax.dot_general(
        hamil, gbar, (((1,), (1,)), ((), ())), preferred_element_type=jnp.float32
    )
    return (d_green, d_chol, d_trial)


def solution(mesh):
    return jax.shard_map(
        shards,
        mesh=mesh,
        in_specs=(
            P(("groups", "walk"), None, None),
            P(("groups", "chol"), None, None),
            P(("groups", "chol"), None),
            P("chol", None),
            P("groups"),
        ),
        out_specs=(
            P(("groups", "walk"), None, "chol"),
            P(("groups", "chol"), None, "walk"),
            P(("groups", "chol"), None),
        ),
        check_vma=False,
    )
```

profile of v0, /device:TPU:0, one launch (start us, length us, event | category | flops | bytes accessed | tf_op | source)
XLA Modules:
  0.0 101.0 jit_solution(4208986423430562566)
XLA Ops:
  7.2 0.0 copy-start
  7.2 0.0 all-gather.2.cloned.1.call-start
  7.2 0.7 all-gather.2.cloned.1.call-update
  7.9 0.0 reduce-scatter.4.cloned.1.call-start
  8.0 1.2 %dynamic_slice.10 = f32[1]{0:T(128)} dynamic-slice(f32[4]{0:T(128)} %param.9, s32[]{:T(128)S(6)} %select_n.7), dynamic_slice_sizes={1} | dynamic-slice | bytes 12 | tf_op jit(solution)/shard_map/dynamic_slice | solution.py:10
  9.2 28.8 %all-gather.2.cloned.1.call-done = bf16[4,200,1600]{2,1,0:T(8,128)(2,1)} async-done(((bf16[1,200,1600]{2,1,0:T(8,128)(2,1)}), bf16[4,200,1600]{2,1,0:T(8,128)(2,1)}) %all-gather.2.cloned.1.call-update) | async-done | bytes 2560016 | tf_op jit(solution)/shard_map/all_gather | solution.py:16
  38.1 5.9 %fusion.14 = f32[2,4]{0,1:T(4,128)S(1)} fusion(bf16[4,200,1600]{2,1,0:T(8,128)(2,1)} %all-gather.2.cloned.1.call-done, bf16[2,200,1600]{2,1,0:T(8,128)(2,1)} %param.6), kind=kOutput, calls=%fused_computation.19 | convolution fusion | flops 5120000 | bytes 3840032 | tf_op jit(solution)/shard_map/cip,wip->cw/dot_general | solution.py:17
  44.0 0.0 copy-done.5
  44.0 1.7 %fusion.9 = bf16[2,4,200,200]{2,3,0,1:T(8,128)(2,1)S(1)} fusion(bf16[4,200,1600]{2,1,0:T(8,128)(2,1)S(1)} %copy-done.5, bf16[2,200,1600]{2,1,0:T(8,128)(2,1)S(1)} %copy-done.1, f32[200,200]{0,1:T(8,128)S(1)} %fusion.23, f32[2,4]{0,1:T(4,128)S(1)} %fusion.14, f32[4]{0:T(128)S(1)} %copy-done.6), kind=kOutput, calls=%fused_computation.13 | convolution fusion | flops 1025280000 | bytes 4640048 | tf_op jit(solution)/shard_map/cip,wjp->cwij/dot_general | solution.py:18
  45.7 0.0 copy-start.2
  45.7 0.6 convolution_bitcast_fusion
  46.3 0.3 copy-done.3
  46.6 0.3 copy-done.2
  46.9 2.3 %fusion.3 = f32[1,200,1600]{2,1,0:T(8,128)} fusion(f32[200,1600]{1,0:T(8,128)S(1)} %convolution_bitcast_fusion, bf16[400,200]{1,0:T(8,128)(2,1)S(1)} %copy-done.2, bf16[400,1600]{1,0:T(8,128)(2,1)S(1)} %copy-done, f32[]{:T(128)} %bitcast.7), kind=kOutput, calls=%fused_computation.5 | convolution fusion | flops 256640000 | bytes 4000004 | tf_op jit(solution)/shard_map/dot_general | solution.py:11
  49.1 4.6 %copy.33 = f32[1,200,1600]{1,0,2:T(1,128)S(1)} copy(f32[1,200,1600]{2,1,0:T(8,128)} %fusion.3) | data formatting | bytes 2560000
  53.8 1.3 %copy.49 = f32[1600,1,200]{2,0,1:T(8,128)} copy(f32[1600,1,200]{2,1,0:T(1,128)S(1)} %bitcast.54) | data formatting | bytes 2560000
  55.0 0.0 reduce-scatter.4.cloned.1.call-update
  55.1 6.2 %fusion.4 = bf16[1,200,1600]{2,0,1:T(2,128)(2,1)S(1)} fusion(bf16[4,200,1600]{2,1,0:T(8,128)(2,1)} %all-gather.2.cloned.1.call-done, f32[4]{0:T(128)S(1)} %copy-done.6), kind=kOutput, calls=%fused_computation.6 | convolution fusion | flops 15360000 | bytes 3200016 | tf_op jit(solution)/shard_map/w,wip->ip/dot_general | solution.py:30
  61.3 0.6 convolution_bitcast_fusion.2
  61.9 0.9 copy.27
  62.8 2.8 %convolution_bitcast_fusion.1 = f32[2,200,400]{2,1,0:T(8,128)} fusion(bf16[2,4,200,200]{2,3,0,1:T(8,128)(2,1)S(1)} %copy-done.4, bf16[4,200,1600]{2,1,0:T(8,128)(2,1)} %all-gather.2.cloned.1.call-done, s32[]{:T(128)S(6)} %select_n.8), kind=kOutput, calls=%fused_computation.17 | convolution fusion | flops 256000000 | bytes 2099204 | tf_op jit(solution)/shard_map/cwji,wjp->cip/dot_general | solution.py:27
  65.6 26.0 %reduce-scatter.4.cloned.1.call-done = f32[400,200]{1,0:T(8,128)} async-done(((f32[1600,200]{1,0:T(8,128)}), f32[400,200]{1,0:T(8,128)}) %reduce-scatter.4.cloned.1.call-update) | async-done | bytes 320016
  91.7 1.3 %reshape_bitcast_fusion = f32[1,200,400]{1,0,2:T(1,128)S(1)} fusion(f32[400,200]{1,0:T(8,128)} %reduce-scatter.4.cloned.1.call-done), kind=kLoop, calls=%fused_computation.22 | loop fusion | bytes 640000
  93.0 1.2 %copy.34 = f32[1,200,400]{2,1,0:T(8,128)} copy(f32[1,200,400]{1,0,2:T(1,128)S(1)} %reshape_bitcast_fusion) | data formatting | bytes 640000
  (10 shorter events, 0.0 us)
Async XLA Ops:
  7.2 39.4 %copy-start = (bf16[400,1600]{1,0:T(8,128)(2,1)S(1)}, bf16[400,1600]{1,0:T(8,128)(2,1)}, u32[]{:S(2)}) copy-start(bf16[400,1600]{1,0:T(8,128)(2,1)} %param.8) | copy-start | bytes 3840004
  7.2 30.9 %all-gather.2.cloned.1.call-start = ((), (), s32[]{:S(2)}) async-start(), calls=%async_computation.1 | async-start | bytes 3328000 | tf_op jit(solution)/shard_map/all_gather | solution.py:16
  7.9 83.8 %reduce-scatter.4.cloned.1.call-start = ((), (), s32[]{:S(2)}) async-start(), calls=%async_computation.2 | async-start | bytes 2048000
  9.2 34.7 %copy-start.1 = (bf16[2,200,1600]{2,1,0:T(8,128)(2,1)S(1)}, bf16[2,200,1600]{2,1,0:T(8,128)(2,1)}, u32[]{:S(2)}) copy-start(bf16[2,200,1600]{2,1,0:T(8,128)(2,1)} %param.6) | copy-start | bytes 3840004
  9.2 34.7 %copy-start.6 = (f32[4]{0:T(128)S(1)}, f32[4]{0:T(128)}, u32[]{:S(2)}) copy-start(f32[4]{0:T(128)} %param.9) | copy-start | bytes 52
  38.1 5.9 %copy-start.5 = (bf16[4,200,1600]{2,1,0:T(8,128)(2,1)S(1)}, bf16[4,200,1600]{2,1,0:T(8,128)(2,1)}, u32[]{:S(2)}) copy-start(bf16[4,200,1600]{2,1,0:T(8,128)(2,1)} %all-gather.2.cloned.1.call-done) | copy-start | bytes 7680004
  45.7 0.9 copy-start.3
  45.7 1.2 %copy-start.2 = (bf16[400,200]{1,0:T(8,128)(2,1)S(1)}, bf16[400,200]{1,0:T(8,128)(2,1)}, u32[]{:S(2)}) copy-start(bf16[400,200]{1,0:T(8,128)(2,1)} %param.7) | copy-start | bytes 480004
  61.3 1.5 %copy-start.4 = (bf16[2,4,200,200]{2,3,0,1:T(8,128)(2,1)S(1)}, bf16[2,4,200,200]{2,3,0,1:T(8,128)(2,1)}, u32[]{:S(2)}) copy-start(bf16[2,4,200,200]{2,3,0,1:T(8,128)(2,1)} %copy-done.3) | copy-start | bytes 1920004
Sparse Core Ops, SparseCore 0:
  9.5 28.4 all-gather.1
  55.2 36.4 reduce-scatter.3
where the time goes:
time: 101 us
  waiting for transfers between devices  55.6 us (55%)
  matrix products  20 us (20%)
  between operations  14.1 us (14%)
  local copies, waits for them, and re-layouts  11.2 us (11%)
    all_gather x1, waiting for transfers between devices, shards(): greens = lax.all_gather(green, 'walk', axis=0, tiled=True)  28.8 us
    unnamed x3, waiting for transfers between devices  26.7 us
    unnamed x19, local copies, waits for them, and re-layouts  9.96 us
    dot_general x1, matrix products, shards(): jnp.einsum('w,wip->ip', energy_cot, greens, precision=lax.Precision.HIGHE...  6.17 us
    dot_general x1, matrix products, shards(): jnp.einsum('cip,wip->cw', chol, greens, preferred_element_type=jnp.float32)  5.9 us
    dot_general x1, matrix products, shards(): jnp.einsum('cwji,wjp->cip', kernel_mat, green_share, preferred_element_ty...  2.85 us
    dot_general x1, matrix products, shards(): lax.dot_general(trial, hamil, (((0,), (0,)), ((), ())), preferred_element...  2.28 us
  transfers between devices with their start and end apart: 2, of which 2 were waited for; matrix products, arithmetic and copies ran while one was open for 12% of the time, Pallas kernels for 0%

commit v1 on v0

--- a/solution.py
+++ b/solution.py
@@ -1,7 +1,204 @@
+import functools
+
 import jax
 import jax.numpy as jnp
 from jax import lax
+from jax.experimental import pallas as pl
+from jax.experimental.pallas import tpu as pltpu
 from jax.sharding import PartitionSpec as P
+
+MESH = pl.DeviceIdType.MESH
+F32 = jnp.float32
+BF16 = jnp.bfloat16
+
+
+def nt(a, b):
+    return lax.dot_general(a, b, (((1,), (1,)), ((), ())), preferred_element_type=F32)
+
+
+def nn(a, b):
+    return lax.dot_general(a, b, (((1,), (0,)), ((), ())), preferred_element_type=F32)
+
+
+def tn(a, b):
+    return lax.dot_general(a, b, (((0,), (0,)), ((), ())), preferred_element_type=F32)
+
+
+def kernel_of(exchange, cot):
+    rows = lax.broadcasted_iota(jnp.int32, exchange.shape, 0)
+    cols = lax.broadcasted_iota(jnp.int32, exchange.shape, 1)
+    diagonal = rows == cols
+    coulomb = jnp.sum(jnp.where(diagonal, exchange, 0.0))
+    return (cot * (jnp.where(diagonal, coulomb, 0.0) - exchange)).astype(BF16)
+
+
+def row_chunks(rows, count):
+    step = -(-rows // count) // 16 * 16
+    starts = [step * k for k in range(count)]
+    return [(s, (rows if k == count - 1 else s + step) - s) for k, s in enumerate(starts)]
+
+
+def body(
+    n_chol, chunks, cot_ref, green_ref, chol_ref, trial_ref, hamil_ref,
+    dgreen_ref, dchol_ref, dtrial_ref,
+    greens, part, mine, outbox, inbox, gbar, green_q,
+    core_send, core_recv, x_send, x_recv, relay_send, relay_recv, z_send, z_recv,
+):
+    walk = lax.axis_index("walk")
+    rank = lax.axis_index("chol")
+    n_walk = 4
+    n_vec = chol_ref.shape[0]
+    peer = [walk, walk + 1 - 2 * (walk % 2), (walk + 2) % n_walk, n_walk - 1 - walk]
+    quarter = dchol_ref.shape[2]
+    third = dgreen_ref.shape[2]
+
+    barrier = pltpu.get_barrier_semaphore()
+    for d in (1, 2):
+        pl.semaphore_signal(barrier, inc=1, device_id={"walk": peer[d]}, device_id_type=MESH)
+    for c in range(1, n_chol):
+        pl.semaphore_signal(
+            barrier, inc=1, device_id={"chol": (rank + c) % n_chol}, device_id_type=MESH
+        )
+    pl.semaphore_wait(barrier, 2 + n_chol - 1)
+
+    def to_core():
+        return pltpu.make_async_remote_copy(
+            green_ref.at[0], greens.at[1], core_send, core_recv,
+            device_id={"walk": peer[1]}, device_id_type=MESH,
+        )
+
+    def to_x(k):
+        span = pl.ds(*chunks[k])
+        return pltpu.make_async_remote_copy(
+            green_ref.at[0, span], greens.at[2, span], x_send.at[k], x_recv.at[k],
+            device_id={"walk": peer[2]}, device_id_type=MESH,
+        )
+
+    def relay(k):
+        span = pl.ds(*chunks[k])
+        return pltpu.make_async_remote_copy(
+            greens.at[2, span], greens.at[3, span], relay_send.at[k], relay_recv.at[k],
+            device_id={"walk": peer[1]}, device_id_type=MESH,
+        )
+
+    def to_z(c):
+        return pltpu.make_async_remote_copy(
+            outbox.at[c], inbox.at[rank], z_send.at[c], z_recv.at[rank],
+            device_id={"chol": c}, device_id_type=MESH,
+        )
+
+    def from_z(c):
+        return pltpu.make_async_remote_copy(
+            outbox.at[c], inbox.at[c], z_send.at[c], z_recv.at[c],
+            device_id={"chol": c}, device_id_type=MESH,
+        )
+
+    for k in range(len(chunks)):
+        to_x(k).start()
+    to_core().start()
+
+    cot = cot_ref[walk]
+    total = cot * tn(trial_ref[...], hamil_ref[...])
+    for g in range(n_vec):
+        total = total + nn(kernel_of(nt(chol_ref[g], green_ref[0]), cot), chol_ref[g])
+    part[...] = total
+    for c in range(n_chol):
+        piece = part[:, c * third:(c + 1) * third]
+
+        @pl.when(rank == c)
+        def _():
+            mine[...] = piece
+
+        @pl.when(rank != c)
+        def _():
+            outbox[c] = piece.astype(BF16)
+            to_z(c).start()
+
+    def absorb(d, green):
+        weight = cot_ref[peer[d]]
+        wide = green.astype(F32)
+        if d == 0:
+            gbar[...] = weight * wide
+        else:
+            gbar[...] += weight * wide
+        for q in range(n_walk):
+
+            @pl.when(walk == q)
+            def _():
+                green_q[...] = wide[:, q * quarter:(q + 1) * quarter].astype(BF16)
+
+        for g in range(n_vec):
+            term = nn(kernel_of(nt(green, chol_ref[g]), weight), green_q[...])
+            if d == 0:
+                dchol_ref[g] = term
+            else:
+                dchol_ref[g] += term
+
+    absorb(0, green_ref[0])
+    for k in range(len(chunks)):
+        if k == 1:
+            to_core().wait_recv()
+            absorb(1, greens[1])
+        to_x(k).wait_recv()
+        relay(k).start()
+    absorb(2, greens[2])
+    for k in range(len(chunks)):
+        relay(k).wait_recv()
+    absorb(3, greens[3])
+    dtrial_ref[...] = nt(hamil_ref[...], gbar[...].astype(BF16))
+
+    for c in range(n_chol):
+
+        @pl.when(rank != c)
+        def _():
+            from_z(c).wait_recv()
+            mine[...] += inbox[c].astype(F32)
+
+    dgreen_ref[0] = mine[...]
+    to_core().wait_send()
+    for k in range(len(chunks)):
+        to_x(k).wait_send()
+        relay(k).wait_send()
+    for c in range(n_chol):
+
+        @pl.when(rank != c)
+        def _():
+            to_z(c).wait_send()
+
+
+def fused(green, chol, trial, hamil, energy_cot):
+    n_chol = lax.axis_size("chol")
+    n_walk = lax.axis_size("walk")
+    _, occ, orb = green.shape
+    chunks = row_chunks(occ, 3)
+    vmem = pl.BlockSpec(memory_space=pltpu.VMEM)
+    dma = pltpu.SemaphoreType.DMA
+    return pl.pallas_call(
+        functools.partial(body, n_chol, chunks),
+        out_shape=(
+            jax.ShapeDtypeStruct((1, occ, orb // n_chol), F32),
+            jax.ShapeDtypeStruct((chol.shape[0], occ, orb // n_walk), F32),
+            jax.ShapeDtypeStruct((hamil.shape[0], occ), F32),
+        ),
+        in_specs=[pl.BlockSpec(memory_space=pltpu.SMEM)] + [vmem] * 4,
+        out_specs=(vmem,) * 3,
+        scratch_shapes=[
+            pltpu.VMEM((n_walk, occ, orb), BF16),
+            pltpu.VMEM((occ, orb), F32),
+            pltpu.VMEM((occ, orb // n_chol), F32),
+            pltpu.VMEM((n_chol, occ, orb // n_chol), BF16),
+            pltpu.VMEM((n_chol, occ, orb // n_chol), BF16),
+            pltpu.VMEM((occ, orb), F32),
+            pltpu.VMEM((occ, orb // n_walk), BF16),
+            dma, dma,
+            dma((len(chunks),)), dma((len(chunks),)),
+            dma((len(chunks),)), dma((len(chunks),)),
+            dma((n_chol,)), dma((n_chol,)),
+        ],
+        compiler_params=pltpu.CompilerParams(
+            collective_id=0, has_side_effects=True, vmem_limit_bytes=60 * 1024 * 1024
+        ),
+    )(energy_cot, green, chol, trial, hamil)
 
 
 def shards(green, chol, trial, hamil, energy_cot):
@@ -41,8 +238,9 @@
 
 
 def solution(mesh):
+    direct = mesh.shape["walk"] == 4 and mesh.shape["chol"] <= 8
     return jax.shard_map(
-        shards,
+        fused if direct else shards,
         mesh=mesh,
         in_specs=(
             P(("groups", "walk"), None, None),

time: 101 us -> 33.1 us (0.33)
  waiting for transfers between devices: 55.6 us -> 0 us
  Pallas kernels: 0 us -> 28.8 us
  matrix products: 20 us -> 0 us
  between operations: 14.1 us -> 0.66 us
  local copies, waits for them, and re-layouts: 11.2 us -> 3.53 us
    all_gather x1 -> x0, waiting for transfers between devices: 28.8 us -> none  [shards(): greens = lax.all_gather(green, 'walk', axis=0, tiled=True)]
    pallas_call x0 -> x1, Pallas kernels: none -> 28.8 us  [fused(): pl.pallas_call(functools.partial(body, n_chol, chunks), out_shape=(jax.Sh...]
    unnamed x3 -> x0, waiting for transfers between devices: 26.7 us -> none
    dot_general x7 -> x0, matrix products: 20 us -> none  [the longest x1 6.17 us: shards(): jnp.einsum('w,wip->ip', energy_cot, greens, precision=lax.Precision.HIGHE...]
    unnamed x19 -> x7, local copies, waits for them, and re-layouts: 9.96 us -> 3.53 us
    dynamic_slice x1 -> x0, local copies, waits for them, and re-layouts: 1.24 us -> none  [shards(): lax.dynamic_slice_in_dim(energy_cot, walk_rank * walk_rows, walk_rows, 0)]
  transfers between devices with their start and end apart: 2 -> 0, of which waited for: 2 -> 0; matrix products, arithmetic and copies ran while one was open for 12% -> 0% of each run, Pallas kernels for 0% -> 0%
where the time goes in v1:
time: 33.1 us; the launch traced here: 33 us
  Pallas kernels  28.8 us (87%)
  local copies, waits for them, and re-layouts  3.53 us (11%)
  between operations  0.66 us (2%)
    pallas_call x1, Pallas kernels, fused(): pl.pallas_call(functools.partial(body, n_chol, chunks), out_shape=(jax.Sh...  28.8 us
    unnamed x7, local copies, waits for them, and re-layouts  3.53 us

profile of v1, /device:TPU:0, one launch (start us, length us, event | category | flops | bytes accessed | tf_op | source)
XLA Modules:
  0.0 33.0 jit_solution(12670994231616537560)
XLA Ops:
  0.6 28.8 %shard_map.76 = (f32[1,200,400]{2,1,0:T(8,128)}, f32[2,200,400]{2,1,0:T(8,128)}, f32[400,200]{1,0:T(8,128)}) custom-call(f32[4]{0:T(128)} %cot_ref.1, bf16[1,200,1600]{2,1,0:T(8,128)(2,1)} %green_ref.1, bf16[2,200,1600]{2,1,0:T(8,128)(2,1)} %chol_ref.1, bf16[400,200]{1,0:T(8,128)(2,1)} %trial_ref.1, bf16[400,1600]{1,0:T(8,128)(2,1)} %hamil_ref.1), custom_call_target="tpu_custom_call" | custom-call | tf_op jit(solution)/shard_map/pallas_call | solution.py:176
  29.4 0.0 copy-start
  29.5 0.0 copy-start.1
  29.5 1.9 %copy.11 = f32[1,200,400]{2,1,0:T(8,128)} copy(f32[1,200,400]{2,1,0:T(8,128)} %get-tuple-element.6) | data formatting | bytes 640000
  31.3 0.0 copy-done
  31.3 0.9 %copy.12 = f32[2,200,400]{2,1,0:T(8,128)} copy(f32[2,200,400]{2,1,0:T(8,128)S(1)} %copy-done) | data formatting | bytes 1280000
  32.2 0.0 copy-done.1
  32.2 0.8 %copy.13 = f32[400,200]{1,0:T(8,128)} copy(f32[400,200]{1,0:T(8,128)S(1)} %copy-done.1) | data formatting | bytes 640000
Async XLA Ops:
  29.4 1.9 %copy-start = (f32[2,200,400]{2,1,0:T(8,128)S(1)}, f32[2,200,400]{2,1,0:T(8,128)}, u32[]{:S(2)}) copy-start(f32[2,200,400]{2,1,0:T(8,128)} %get-tuple-element.7) | copy-start | bytes 1920004
  29.5 2.8 %copy-start.1 = (f32[400,200]{1,0:T(8,128)S(1)}, f32[400,200]{1,0:T(8,128)}, u32[]{:S(2)}) copy-start(f32[400,200]{1,0:T(8,128)} %get-tuple-element.8) | copy-start | bytes 960004

commit v2 on v1

--- a/solution.py
+++ b/solution.py
@@ -39,10 +39,12 @@
 
 
 def body(
-    n_chol, chunks, cot_ref, green_ref, chol_ref, trial_ref, hamil_ref,
+    n_chol, chunks, cot_ref, green_hbm, chol_hbm, trial_hbm, hamil_hbm,
     dgreen_ref, dchol_ref, dtrial_ref,
-    greens, part, mine, outbox, inbox, gbar, green_q,
-    core_send, core_recv, x_send, x_recv, relay_send, relay_recv, z_send, z_recv,
+    green_ref, chol_ref, trial_ref, hamil_ref,
+    greens, held, outbox, inbox, foldbox, gbar, green_q, kernels,
+    load_sem, core_send, core_recv, x_send, x_recv, relay_send, relay_recv,
+    z_send, z_recv, fold_recv,
 ):
     walk = lax.axis_index("walk")
     rank = lax.axis_index("chol")
@@ -51,6 +53,9 @@
     peer = [walk, walk + 1 - 2 * (walk % 2), (walk + 2) % n_walk, n_walk - 1 - walk]
     quarter = dchol_ref.shape[2]
     third = dgreen_ref.shape[2]
+    orb = green_ref.shape[1]
+    last = n_chol - 1
+    folds = {(0, last): 1, (last, 0): last - 1} if n_chol == 4 else {}
 
     barrier = pltpu.get_barrier_semaphore()
     for d in (1, 2):
@@ -59,18 +64,27 @@
         pl.semaphore_signal(
             barrier, inc=1, device_id={"chol": (rank + c) % n_chol}, device_id_type=MESH
         )
+    loads = [
+        pltpu.make_async_copy(source, target, load_sem.at[k])
+        for k, (source, target) in enumerate((
+            (green_hbm.at[0], green_ref), (chol_hbm, chol_ref),
+            (trial_hbm, trial_ref), (hamil_hbm, hamil_ref),
+        ))
+    ]
+    for load in loads:
+        load.start()
     pl.semaphore_wait(barrier, 2 + n_chol - 1)
 
     def to_core():
         return pltpu.make_async_remote_copy(
-            green_ref.at[0], greens.at[1], core_send, core_recv,
+            green_hbm.at[0], greens.at[1], core_send, core_recv,
             device_id={"walk": peer[1]}, device_id_type=MESH,
         )
 
     def to_x(k):
         span = pl.ds(*chunks[k])
         return pltpu.make_async_remote_copy(
-            green_ref.at[0, span], greens.at[2, span], x_send.at[k], x_recv.at[k],
+            green_hbm.at[0, span], greens.at[2, span], x_send.at[k], x_recv.at[k],
             device_id={"walk": peer[2]}, device_id_type=MESH,
         )
 
@@ -91,6 +105,12 @@
         return pltpu.make_async_remote_copy(
             outbox.at[c], inbox.at[c], z_send.at[c], z_recv.at[c],
             device_id={"chol": c}, device_id_type=MESH,
+        )
+
+    def to_fold(c, middle):
+        return pltpu.make_async_remote_copy(
+            outbox.at[c], foldbox, z_send.at[c], fold_recv,
+            device_id={"chol": middle}, device_id_type=MESH,
         )
 
     for k in range(len(chunks)):
@@ -98,21 +118,33 @@
     to_core().start()
 
     cot = cot_ref[walk]
-    total = cot * tn(trial_ref[...], hamil_ref[...])
+    loads[0].wait()
+    loads[1].wait()
     for g in range(n_vec):
-        total = total + nn(kernel_of(nt(chol_ref[g], green_ref[0]), cot), chol_ref[g])
-    part[...] = total
-    for c in range(n_chol):
-        piece = part[:, c * third:(c + 1) * third]
-
-        @pl.when(rank == c)
-        def _():
-            mine[...] = piece
-
-        @pl.when(rank != c)
-        def _():
-            outbox[c] = piece.astype(BF16)
-            to_z(c).start()
+        kernels[g] = kernel_of(nt(chol_ref[g], green_ref[...]), cot)
+    loads[2].wait()
+    loads[3].wait()
+    for c in [last] + list(range(last)):
+        low = c * third // 128 * 128
+        high = min(orb, -(-(c + 1) * third // 128) * 128)
+        window = cot * tn(trial_ref[...], hamil_ref[:, low:high])
+        for g in range(n_vec):
+            window = window + nn(kernels[g], chol_ref[g, :, low:high])
+        piece = window[:, c * third - low:(c + 1) * third - low]
+        for r in range(n_chol):
+
+            @pl.when(rank == r)
+            def _():
+                if r == c:
+                    dgreen_ref[0] = piece
+                elif (r, c) in folds:
+                    outbox[c] = piece.astype(BF16)
+                    to_fold(c, folds[r, c]).start()
+                elif any(end == c and folds[start, end] == r for start, end in folds):
+                    held[...] = piece
+                else:
+                    outbox[c] = piece.astype(BF16)
+                    to_z(c).start()
 
     def absorb(d, green):
         weight = cot_ref[peer[d]]
@@ -134,7 +166,15 @@
             else:
                 dchol_ref[g] += term
 
-    absorb(0, green_ref[0])
+    absorb(0, green_ref[...])
+    for (start, end), middle in folds.items():
+
+        @pl.when(rank == middle)
+        def _():
+            to_fold(end, middle).wait_recv()
+            outbox[end] = (held[...] + foldbox[...].astype(F32)).astype(BF16)
+            to_z(end).start()
+
     for k in range(len(chunks)):
         if k == 1:
             to_core().wait_recv()
@@ -147,14 +187,15 @@
     absorb(3, greens[3])
     dtrial_ref[...] = nt(hamil_ref[...], gbar[...].astype(BF16))
 
-    for c in range(n_chol):
-
-        @pl.when(rank != c)
+    for r in range(n_chol):
+
+        @pl.when(rank == r)
         def _():
-            from_z(c).wait_recv()
-            mine[...] += inbox[c].astype(F32)
-
-    dgreen_ref[0] = mine[...]
+            for c in range(n_chol):
+                if c != r and (c, r) not in folds:
+                    from_z(c).wait_recv()
+                    dgreen_ref[0] += inbox[c].astype(F32)
+
     to_core().wait_send()
     for k in range(len(chunks)):
         to_x(k).wait_send()
@@ -164,6 +205,15 @@
         @pl.when(rank != c)
         def _():
             to_z(c).wait_send()
+
+
+def write_out(*refs):
+    sources, targets, sem = refs[:3], refs[3:6], refs[6]
+    copies = [pltpu.make_async_copy(s, t, sem.at[k]) for k, (s, t) in enumerate(zip(sources, targets))]
+    for copy in copies:
+        copy.start()
+    for copy in copies:
+        copy.wait()
 
 
 def fused(green, chol, trial, hamil, energy_cot):
@@ -172,33 +222,48 @@
     _, occ, orb = green.shape
     chunks = row_chunks(occ, 3)
     vmem = pl.BlockSpec(memory_space=pltpu.VMEM)
+    anywhere = pl.BlockSpec(memory_space=pl.ANY)
     dma = pltpu.SemaphoreType.DMA
-    return pl.pallas_call(
+    shapes = [
+        (1, occ, orb // n_chol),
+        (chol.shape[0], occ, orb // n_walk),
+        (hamil.shape[0], occ),
+    ]
+    results = pl.pallas_call(
         functools.partial(body, n_chol, chunks),
-        out_shape=(
-            jax.ShapeDtypeStruct((1, occ, orb // n_chol), F32),
-            jax.ShapeDtypeStruct((chol.shape[0], occ, orb // n_walk), F32),
-            jax.ShapeDtypeStruct((hamil.shape[0], occ), F32),
-        ),
-        in_specs=[pl.BlockSpec(memory_space=pltpu.SMEM)] + [vmem] * 4,
+        out_shape=tuple(pltpu.VMEM(shape, F32) for shape in shapes),
+        in_specs=[pl.BlockSpec(memory_space=pltpu.SMEM)] + [anywhere] * 4,
         out_specs=(vmem,) * 3,
         scratch_shapes=[
+            pltpu.VMEM((occ, orb), BF16),
+            pltpu.VMEM(chol.shape, BF16),
+            pltpu.VMEM(trial.shape, BF16),
+            pltpu.VMEM(hamil.shape, BF16),
             pltpu.VMEM((n_walk, occ, orb), BF16),
-            pltpu.VMEM((occ, orb), F32),
             pltpu.VMEM((occ, orb // n_chol), F32),
             pltpu.VMEM((n_chol, occ, orb // n_chol), BF16),
             pltpu.VMEM((n_chol, occ, orb // n_chol), BF16),
+            pltpu.VMEM((occ, orb // n_chol), BF16),
             pltpu.VMEM((occ, orb), F32),
             pltpu.VMEM((occ, orb // n_walk), BF16),
-            dma, dma,
+            pltpu.VMEM((chol.shape[0], occ, occ), BF16),
+            dma((4,)), dma, dma,
             dma((len(chunks),)), dma((len(chunks),)),
             dma((len(chunks),)), dma((len(chunks),)),
-            dma((n_chol,)), dma((n_chol,)),
+            dma((n_chol,)), dma((n_chol,)), dma,
         ],
         compiler_params=pltpu.CompilerParams(
             collective_id=0, has_side_effects=True, vmem_limit_bytes=60 * 1024 * 1024
         ),
     )(energy_cot, green, chol, trial, hamil)
+    return pl.pallas_call(
+        write_out,
+        out_shape=tuple(jax.ShapeDtypeStruct(shape, F32) for shape in shapes),
+        in_specs=[anywhere] * 3,
+        out_specs=(anywhere,) * 3,
+        scratch_shapes=[dma((3,))],
+        compiler_params=pltpu.CompilerParams(vmem_limit_bytes=1024 * 1024),
+    )(*results)
 
 
 def shards(green, chol, trial, hamil, energy_cot):

time: 33.1 us -> 28.5 us (0.86)
  local copies, waits for them, and re-layouts: 3.53 us -> 0 us
  Pallas kernels: 28.8 us -> 27.7 us
    unnamed x7 -> x0, local copies, waits for them, and re-layouts: 3.53 us -> none
    pallas_call x1 -> x2, Pallas kernels: 28.8 us -> 27.7 us  [the longest x1 26.5 us: fused(): pl.pallas_call(functools.partial(body, n_chol, chunks), out_shape=tuple((...]
where the time goes in v2:
time: 28.5 us; the launch traced here: 28.3 us
  Pallas kernels  27.7 us (97%)
  between operations  0.64 us (2%)
    pallas_call x1, Pallas kernels, fused(): pl.pallas_call(functools.partial(body, n_chol, chunks), out_shape=tuple((...  26.5 us
    pallas_call x1, Pallas kernels, fused(): pl.pallas_call(write_out, out_shape=tuple((jax.ShapeDtypeStruct(shape, F3...  1.19 us

profile of v2, /device:TPU:0, one launch (start us, length us, event | category | flops | bytes accessed | tf_op | source)
XLA Modules:
  0.0 28.3 jit_solution(17914605131888154257)
XLA Ops:
  0.6 26.5 %shard_map.76 = (f32[1,200,400]{2,1,0:T(8,128)S(1)}, f32[2,200,400]{2,1,0:T(8,128)S(1)}, f32[400,200]{1,0:T(8,128)S(1)}) custom-call(f32[4]{0:T(128)} %cot_ref.1, bf16[1,200,1600]{2,1,0:T(8,128)(2,1)} %green_hbm.1, bf16[2,200,1600]{2,1,0:T(8,128)(2,1)} %chol_hbm.1, bf16[400,200]{1,0:T(8,128)(2,1)} %trial_hbm.1, bf16[400,1600]{1,0:T(8,128)(2,1)} %hamil_hbm.1), custom_call_target="tpu_custom_call" | custom-call | tf_op jit(solution)/shard_map/pallas_call | solution.py:232
  27.1 1.2 %shard_map.77 = (f32[1,200,400]{2,1,0:T(8,128)}, f32[2,200,400]{2,1,0:T(8,128)}, f32[400,200]{1,0:T(8,128)}) custom-call(f32[1,200,400]{2,1,0:T(8,128)S(1)} %get-tuple-element.6.refs_0_, f32[2,200,400]{2,1,0:T(8,128)S(1)} %get-tuple-element.7.refs_1_, f32[400,200]{1,0:T(8,128)S(1)} %get-tuple-element.8.refs_2_), custom_call_target="tpu_custom_call" | custom-call | tf_op jit(solution)/shard_map/pallas_call | solution.py:259

commit v3 on v2

--- a/solution.py
+++ b/solution.py
@@ -32,19 +32,19 @@
     return (cot * (jnp.where(diagonal, coulomb, 0.0) - exchange)).astype(BF16)
 
 
-def row_chunks(rows, count):
-    step = -(-rows // count) // 16 * 16
-    starts = [step * k for k in range(count)]
-    return [(s, (rows if k == count - 1 else s + step) - s) for k, s in enumerate(starts)]
+def row_chunks(rows):
+    step = -(-rows // 3) // 16 * 16
+    starts = [0, step * 3 // 2 // 16 * 16, 2 * step, 2 * step + step // 2 // 16 * 16]
+    return [(s, e - s) for s, e in zip(starts, starts[1:] + [rows])]
 
 
 def body(
     n_chol, chunks, cot_ref, green_hbm, chol_hbm, trial_hbm, hamil_hbm,
     dgreen_ref, dchol_ref, dtrial_ref,
     green_ref, chol_ref, trial_ref, hamil_ref,
-    greens, held, outbox, inbox, foldbox, gbar, green_q, kernels,
+    greens, held, outbox, inbox, foldbox, gbar, green_q, kernels, partial_ex,
     load_sem, core_send, core_recv, x_send, x_recv, relay_send, relay_recv,
-    z_send, z_recv, fold_recv,
+    z_send, z_recv, fold_recv, pair_send, pair_recv,
 ):
     walk = lax.axis_index("walk")
     rank = lax.axis_index("chol")
@@ -113,7 +113,20 @@
             device_id={"chol": middle}, device_id_type=MESH,
         )
 
-    for k in range(len(chunks)):
+    def to_pair(k):
+        span = pl.ds(*chunks[k])
+        return pltpu.make_async_remote_copy(
+            greens.at[2, span], greens.at[2, span], pair_send, pair_recv,
+            device_id={"chol": rank + 1 - 2 * (rank % 2)}, device_id_type=MESH,
+        )
+
+    for parity in range(2):
+
+        @pl.when(rank % 2 == parity)
+        def _():
+            to_x(2 + parity).start()
+
+    for k in range(2):
         to_x(k).start()
     to_core().start()
 
@@ -124,7 +137,16 @@
         kernels[g] = kernel_of(nt(chol_ref[g], green_ref[...]), cot)
     loads[2].wait()
     loads[3].wait()
-    for c in [last] + list(range(last)):
+    for turn, c in enumerate([last] + list(range(last))):
+        if turn == 2:
+            for parity in range(2):
+
+                @pl.when(rank % 2 == parity)
+                def _():
+                    to_x(2 + parity).wait_recv()
+                    to_pair(2 + parity).start()
+                    relay(2 + parity).start()
+
         low = c * third // 128 * 128
         high = min(orb, -(-(c + 1) * third // 128) * 128)
         window = cot * tn(trial_ref[...], hamil_ref[:, low:high])
@@ -146,27 +168,36 @@
                     outbox[c] = piece.astype(BF16)
                     to_z(c).start()
 
-    def absorb(d, green):
+    def absorb_rows(d, green, rows):
         weight = cot_ref[peer[d]]
         wide = green.astype(F32)
         if d == 0:
-            gbar[...] = weight * wide
+            gbar[rows, :] = weight * wide
         else:
-            gbar[...] += weight * wide
+            gbar[rows, :] += weight * wide
         for q in range(n_walk):
 
             @pl.when(walk == q)
             def _():
-                green_q[...] = wide[:, q * quarter:(q + 1) * quarter].astype(BF16)
+                green_q[d % 2, rows, :] = wide[:, q * quarter:(q + 1) * quarter].astype(BF16)
 
         for g in range(n_vec):
-            term = nn(kernel_of(nt(green, chol_ref[g]), weight), green_q[...])
+            partial_ex[d % 2, g, rows, :] = nt(green, chol_ref[g])
+
+    def finish(d):
+        for g in range(n_vec):
+            term = nn(kernel_of(partial_ex[d % 2, g], cot_ref[peer[d]]), green_q[d % 2])
             if d == 0:
                 dchol_ref[g] = term
             else:
                 dchol_ref[g] += term
 
-    absorb(0, green_ref[...])
+    def trial_columns(low, high):
+        dtrial_ref[:, low:high] = nt(hamil_ref[...], gbar[low:high, :].astype(BF16))
+
+    every = pl.ds(0, green_ref.shape[0])
+    absorb_rows(0, green_ref[...], every)
+    finish(0)
     for (start, end), middle in folds.items():
 
         @pl.when(rank == middle)
@@ -175,17 +206,35 @@
             outbox[end] = (held[...] + foldbox[...].astype(F32)).astype(BF16)
             to_z(end).start()
 
-    for k in range(len(chunks)):
-        if k == 1:
-            to_core().wait_recv()
-            absorb(1, greens[1])
+    to_core().wait_recv()
+    absorb_rows(1, greens[1], every)
+    finish(1)
+    split = chunks[2][0]
+    rows = green_ref.shape[0]
+    rest = pl.ds(split, rows - split)
+    for parity in range(2):
+
+        @pl.when(rank % 2 == parity)
+        def _():
+            to_pair(3 - parity).wait_recv()
+            relay(3 - parity).start()
+
+    absorb_rows(2, greens[2, rest], rest)
+    relay(2).wait_recv()
+    relay(3).wait_recv()
+    absorb_rows(3, greens[3, rest], rest)
+    trial_columns(split, rows)
+    for k in range(2):
+        span = pl.ds(*chunks[k])
         to_x(k).wait_recv()
         relay(k).start()
-    absorb(2, greens[2])
-    for k in range(len(chunks)):
+        absorb_rows(2, greens[2, span], span)
+        if k == 1:
+            finish(2)
         relay(k).wait_recv()
-    absorb(3, greens[3])
-    dtrial_ref[...] = nt(hamil_ref[...], gbar[...].astype(BF16))
+        absorb_rows(3, greens[3, span], span)
+    finish(3)
+    trial_columns(0, split)
 
     for r in range(n_chol):
 
@@ -198,8 +247,16 @@
 
     to_core().wait_send()
     for k in range(len(chunks)):
+        relay(k).wait_send()
+    for k in range(2):
         to_x(k).wait_send()
-        relay(k).wait_send()
+    for parity in range(2):
+
+        @pl.when(rank % 2 == parity)
+        def _():
+            to_x(2 + parity).wait_send()
+            to_pair(2 + parity).wait_send()
+
     for c in range(n_chol):
 
         @pl.when(rank != c)
@@ -220,7 +277,7 @@
     n_chol = lax.axis_size("chol")
     n_walk = lax.axis_size("walk")
     _, occ, orb = green.shape
-    chunks = row_chunks(occ, 3)
+    chunks = row_chunks(occ)
     vmem = pl.BlockSpec(memory_space=pltpu.VMEM)
     anywhere = pl.BlockSpec(memory_space=pl.ANY)
     dma = pltpu.SemaphoreType.DMA
@@ -245,12 +302,13 @@
             pltpu.VMEM((n_chol, occ, orb // n_chol), BF16),
             pltpu.VMEM((occ, orb // n_chol), BF16),
             pltpu.VMEM((occ, orb), F32),
-            pltpu.VMEM((occ, orb // n_walk), BF16),
+            pltpu.VMEM((2, occ, orb // n_walk), BF16),
             pltpu.VMEM((chol.shape[0], occ, occ), BF16),
+            pltpu.VMEM((2, chol.shape[0], occ, occ), F32),
             dma((4,)), dma, dma,
             dma((len(chunks),)), dma((len(chunks),)),
             dma((len(chunks),)), dma((len(chunks),)),
-            dma((n_chol,)), dma((n_chol,)), dma,
+            dma((n_chol,)), dma((n_chol,)), dma, dma, dma,
         ],
         compiler_params=pltpu.CompilerParams(
             collective_id=0, has_side_effects=True, vmem_limit_bytes=60 * 1024 * 1024
@@ -303,7 +361,7 @@
 
 
 def solution(mesh):
-    direct = mesh.shape["walk"] == 4 and mesh.shape["chol"] <= 8
+    direct = mesh.shape["walk"] == 4 and mesh.shape["chol"] in (2, 4, 6, 8)
     return jax.shard_map(
         fused if direct else shards,
         mesh=mesh,

time: 28.5 us -> 27.3 us (0.958)
  Pallas kernels: 27.7 us -> 26.5 us
    pallas_call x1, Pallas kernels: 26.5 us -> 25.3 us  [fused(): pl.pallas_call(functools.partial(body, n_chol, chunks), out_shape=tuple((...]
where the time goes in v3:
time: 27.3 us; the launch traced here: 27.1 us
  Pallas kernels  26.5 us (97%)
  between operations  0.64 us (2%)
    pallas_call x1, Pallas kernels, fused(): pl.pallas_call(functools.partial(body, n_chol, chunks), out_shape=tuple((...  25.3 us
    pallas_call x1, Pallas kernels, fused(): pl.pallas_call(write_out, out_shape=tuple((jax.ShapeDtypeStruct(shape, F3...  1.19 us

profile of v3, /device:TPU:0, one launch (start us, length us, event | category | flops | bytes accessed | tf_op | source)
XLA Modules:
  0.0 27.1 jit_solution(2707066881808263724)
XLA Ops:
  0.6 25.3 %shard_map.76 = (f32[1,200,400]{2,1,0:T(8,128)S(1)}, f32[2,200,400]{2,1,0:T(8,128)S(1)}, f32[400,200]{1,0:T(8,128)S(1)}) custom-call(f32[4]{0:T(128)} %cot_ref.1, bf16[1,200,1600]{2,1,0:T(8,128)(2,1)} %green_hbm.1, bf16[2,200,1600]{2,1,0:T(8,128)(2,1)} %chol_hbm.1, bf16[400,200]{1,0:T(8,128)(2,1)} %trial_hbm.1, bf16[400,1600]{1,0:T(8,128)(2,1)} %hamil_hbm.1), custom_call_target="tpu_custom_call" | custom-call | tf_op jit(solution)/shard_map/pallas_call | solution.py:289
  26.0 1.2 %shard_map.77 = (f32[1,200,400]{2,1,0:T(8,128)}, f32[2,200,400]{2,1,0:T(8,128)}, f32[400,200]{1,0:T(8,128)}) custom-call(f32[1,200,400]{2,1,0:T(8,128)S(1)} %get-tuple-element.6.refs_0_, f32[2,200,400]{2,1,0:T(8,128)S(1)} %get-tuple-element.7.refs_1_, f32[400,200]{1,0:T(8,128)S(1)} %get-tuple-element.8.refs_2_), custom_call_target="tpu_custom_call" | custom-call | tf_op jit(solution)/shard_map/pallas_call | solution.py:317

commit v4 on v3

--- a/solution.py
+++ b/solution.py
@@ -77,14 +77,14 @@
 
     def to_core():
         return pltpu.make_async_remote_copy(
-            green_hbm.at[0], greens.at[1], core_send, core_recv,
+            green_ref, greens.at[1], core_send, core_recv,
             device_id={"walk": peer[1]}, device_id_type=MESH,
         )
 
     def to_x(k):
         span = pl.ds(*chunks[k])
         return pltpu.make_async_remote_copy(
-            green_hbm.at[0, span], greens.at[2, span], x_send.at[k], x_recv.at[k],
+            green_ref.at[span], greens.at[2, span], x_send.at[k], x_recv.at[k],
             device_id={"walk": peer[2]}, device_id_type=MESH,
         )
 
@@ -120,6 +120,7 @@
             device_id={"chol": rank + 1 - 2 * (rank % 2)}, device_id_type=MESH,
         )
 
+    loads[0].wait()
     for parity in range(2):
 
         @pl.when(rank % 2 == parity)
@@ -131,7 +132,6 @@
     to_core().start()
 
     cot = cot_ref[walk]
-    loads[0].wait()
     loads[1].wait()
     for g in range(n_vec):
         kernels[g] = kernel_of(nt(chol_ref[g], green_ref[...]), cot)

time: 27.3 us -> 27.1 us (level)
  no operation moved by 1% of the time
where the time goes in v4:
time: 27.1 us; the launch traced here: 26.9 us
  Pallas kernels  26.3 us (97%)
  between operations  0.64 us (2%)
    pallas_call x1, Pallas kernels, fused(): pl.pallas_call(functools.partial(body, n_chol, chunks), out_shape=tuple((...  25.1 us
    pallas_call x1, Pallas kernels, fused(): pl.pallas_call(write_out, out_shape=tuple((jax.ShapeDtypeStruct(shape, F3...  1.19 us

profile of v4, /device:TPU:0, one launch (start us, length us, event | category | flops | bytes accessed | tf_op | source)
XLA Modules:
  0.0 26.9 jit_solution(1628113713414706125)
XLA Ops:
  0.6 25.1 %shard_map.76 = (f32[1,200,400]{2,1,0:T(8,128)S(1)}, f32[2,200,400]{2,1,0:T(8,128)S(1)}, f32[400,200]{1,0:T(8,128)S(1)}) custom-call(f32[4]{0:T(128)} %cot_ref.1, bf16[1,200,1600]{2,1,0:T(8,128)(2,1)} %green_hbm.1, bf16[2,200,1600]{2,1,0:T(8,128)(2,1)} %chol_hbm.1, bf16[400,200]{1,0:T(8,128)(2,1)} %trial_hbm.1, bf16[400,1600]{1,0:T(8,128)(2,1)} %hamil_hbm.1), custom_call_target="tpu_custom_call" | custom-call | tf_op jit(solution)/shard_map/pallas_call | solution.py:289
  25.7 1.2 %shard_map.77 = (f32[1,200,400]{2,1,0:T(8,128)}, f32[2,200,400]{2,1,0:T(8,128)}, f32[400,200]{1,0:T(8,128)}) custom-call(f32[1,200,400]{2,1,0:T(8,128)S(1)} %get-tuple-element.6.refs_0_, f32[2,200,400]{2,1,0:T(8,128)S(1)} %get-tuple-element.7.refs_1_, f32[400,200]{1,0:T(8,128)S(1)} %get-tuple-element.8.refs_2_), custom_call_target="tpu_custom_call" | custom-call | tf_op jit(solution)/shard_map/pallas_call | solution.py:317
